TPU v7x, 32 devices: a whole 2x2x4 slice. The times are simulated.
32 devices in a mesh: trial: 16 (over z, y, x), factor: 2 (over core).
Axes of the slice: x: 2, y: 2, z: 4, core: 2. Of those that a mesh axis runs over, the one named last changes fastest.
Arguments:
- observed: float32 [64, 32, 128], P('trial'), may hold values from -6 to 6
- trial_mean: float32 [64], P('trial'), may hold values from -4 to 4
- correlations: float32 [64, 2], P('trial'), may hold values from 0.1 to 0.7
- noise_var: float32 [64], P('trial'), may hold values from 2 to 8
- plot_slot: int32 [64, 32, 128], P('trial'), may hold values from 0 to 2047
- row_count: int32 [64], P('trial'), may hold values from 8 to 32, as said below
- col_count: int32 [64], P('trial'), may hold values from 64 to 128, as said below
- panel_list: int32 [64, 16], P('trial'), may hold values from 0 to 191, as said below
- scores: bfloat16 [128, 24576], P('factor', 'trial'), may hold values from -0.5 to 0.5
- loadings: float32 [64, 128], P('trial', 'factor'), may hold values from -5 to 5
- score_precision: float32 [128], P('factor'), may hold values from 20 to 80
Outputs:
- score_gradient: float32 [128, 24576], P('factor', 'trial')
- loading_gradient: float32 [64, 128], P('trial', 'factor')
Inputs may be any that keep to these rules, and one draw needn't show every extreme that they name: `panel_list`: panel p is owned by index p // 12 of trial. Among the 64 entries of each aligned block of 4 trials, no owner holds more than 8 of them, and in every block some owner holds exactly that many. Entries may repeat. `row_count`: the first trial uses all 32 rows. `col_count`: the first trial uses all 128 columns.
All inputs are finite; a program needn't handle non-finite values.
Results may differ from a plain program's by a relative error of at most 0.0023.
Values may be sent and summed in bfloat16 or wider, within the bound.
A program may use at most 64 MiB of HBM per device.

v0:
```python
import jax
import jax.numpy as jnp
from jax import lax
from jax.sharding import PartitionSpec as P

PANEL = 128
score_step = 0.005
load_step = 0.02


def sweep_axis(values_in, corr_value, position, limit_count, axis_number):
    factor_scale = 1.0 / (1.0 - corr_value * corr_value)
    interior = ((position > 0) & (position < limit_count - 1)).astype(values_in.dtype)
    padding = [(0, 0)] * values_in.ndim
    padding[axis_number] = (1, 1)
    padded = jnp.pad(values_in, padding)
    length = values_in.shape[axis_number]
    lower_side = lax.slice_in_dim(padded, 0, length, axis=axis_number)
    upper_side = lax.slice_in_dim(padded, 2, length + 2, axis=axis_number)
    result = factor_scale * (
        (1.0 + corr_value * corr_value * interior) * values_in
        - corr_value * (lower_side + upper_side)
    )
    return jnp.where(position < limit_count, result, 0.0)


def body(
    observed,
    trial_mean,
    correlations,
    noise_var,
    plot_slot,
    row_count,
    col_count,
    panel_list,
    scores,
    loadings,
    score_precision,
):
    trial_count = lax.axis_size("trial")
    per_dev = panel_list.shape[0]
    per_trial = panel_list.shape[1]
    required_count = per_dev * per_trial
    most_count = 2 * required_count // trial_count
    slots_total = trial_count * most_count
    latent_factor_count = scores.shape[0]
    owned_panels = scores.shape[1] // PANEL
    slots_trial = per_trial * PANEL
    wanted = panel_list.reshape(required_count)
    owner_of = wanted // owned_panels
    local_of = wanted - owner_of * owned_panels
    later_pos = lax.broadcasted_iota(jnp.int32, (required_count, required_count), 0)
    other_pos = lax.broadcasted_iota(jnp.int32, (required_count, required_count), 1)
    earlier = (owner_of[None, :] == owner_of[:, None]) & (other_pos < later_pos)
    rank_of = jnp.sum(earlier.astype(jnp.int32), axis=1)
    position = owner_of * most_count + rank_of
    placer_int = (
        position[None, :] == lax.broadcasted_iota(jnp.int32, (slots_total, required_count), 0)
    ).astype(jnp.int32)
    request = jnp.sum(placer_int * (local_of[None, :] + 1), axis=1) - 1
    placer = placer_int.astype(jnp.float32)
    incoming = lax.all_to_all(request, "trial", split_axis=0, concat_axis=0, tiled=True)
    picker = (
        incoming[None, :] == lax.broadcasted_iota(jnp.int32, (owned_panels, slots_total), 0)
    ).astype(jnp.float32)
    grid_shape = observed.shape
    plot_count = grid_shape[1] * grid_shape[2]
    row_index = lax.broadcasted_iota(jnp.int32, grid_shape, 1)
    col_index = lax.broadcasted_iota(jnp.int32, grid_shape, 2)
    row_upper_limit = row_count[:, None, None]
    col_limit = col_count[:, None, None]
    active = (row_index < row_upper_limit) & (col_index < col_limit)
    flat_slot = plot_slot.reshape(per_dev, plot_count)
    panel_of_plot = flat_slot // PANEL
    cell_of_plot = flat_slot - panel_of_plot * PANEL
    panel_onehot_matrix = (
        panel_of_plot[:, :, None]
        == lax.broadcasted_iota(jnp.int32, (per_dev, plot_count, per_trial), 2)
    ).astype(jnp.float32)
    cell_match = cell_of_plot[:, :, None] == lax.broadcasted_iota(
        jnp.int32, (per_dev, plot_count, PANEL), 2
    )
    correlation_row_values = correlations[:, 0][:, None, None]
    corr_cols = correlations[:, 1][:, None, None]

    def fetch(current):
        whole = lax.all_gather(current, "trial", axis=1, tiled=True)
        grouped = whole.reshape(latent_factor_count, -1, PANEL)
        panel_total = grouped.shape[1]
        chooser = (
            wanted[None, :] == lax.broadcasted_iota(jnp.int32, (panel_total, required_count), 0)
        ).astype(jnp.bfloat16)
        picked = jnp.einsum(
            "kqc,qn->knc", grouped, chooser, preferred_element_type=jnp.float32
        ).astype(jnp.bfloat16)
        return picked.reshape(latent_factor_count, per_dev, slots_trial)

    def evaluate(current, loads_now):
        table = fetch(current)
        table_wide = table.astype(jnp.float32)
        partial_effect = jnp.einsum(
            "ktn,tk->tn", table_wide, loads_now, precision=lax.Precision.HIGHEST
        )
        effect = lax.psum(partial_effect, "factor")
        effect_table_grid = effect.reshape(per_dev, per_trial, PANEL)
        rows_picked = jnp.einsum(
            "jwo,jom->jwm", panel_onehot_matrix, effect_table_grid, precision=lax.Precision.HIGHEST
        )
        fitted = jnp.sum(jnp.where(cell_match, rows_picked, 0.0), axis=2).reshape(grid_shape)
        residual = jnp.where(active, observed - trial_mean[:, None, None] - fitted, 0.0)
        across = sweep_axis(residual, corr_cols, col_index, col_limit, 2)
        weighted = (
            sweep_axis(across, correlation_row_values, row_index, row_upper_limit, 1)
            / noise_var[:, None, None]
        )
        dispersion_amount = jnp.where(
            cell_match, weighted.reshape(per_dev, plot_count)[:, :, None], 0.0
        )
        slot_weight = jnp.einsum(
            "boy,bom->bym", panel_onehot_matrix, dispersion_amount, precision=lax.Precision.HIGHEST
        ).reshape(per_dev, slots_trial)
        load_grad = -jnp.einsum(
            "ktn,tn->tk", table_wide, slot_weight, precision=lax.Precision.HIGHEST
        )
        returned = -(loads_now.T[:, :, None] * slot_weight[None, :, :])
        returned = returned.reshape(latent_factor_count, required_count, PANEL)
        outgoing = jnp.einsum("jn,knc->kjc", placer, returned, precision=lax.Precision.HIGHEST)
        arrived = lax.all_to_all(outgoing, "trial", split_axis=1, concat_axis=1, tiled=True)
        summed = jnp.einsum("qj,kjc->kqc", picker, arrived, precision=lax.Precision.HIGHEST)
        score_grad = score_precision[:, None] * current.astype(jnp.float32) + summed.reshape(
            latent_factor_count, owned_panels * PANEL
        )
        return (score_grad, load_grad)

    first_scores, first_loads = evaluate(scores, loadings)
    new_scores = (scores.astype(jnp.float32) - score_step * first_scores).astype(jnp.bfloat16)
    new_loads = loadings - load_step * first_loads
    return evaluate(new_scores, new_loads)


def solution(mesh):
    in_specs = (
        P("trial", None, None),
        P("trial"),
        P("trial", None),
        P("trial"),
        P("trial", None, None),
        P("trial"),
        P("trial"),
        P("trial", None),
        P("factor", "trial"),
        P("trial", "factor"),
        P("factor"),
    )
    out_specs = (P("factor", "trial"), P("trial", "factor"))
    return jax.shard_map(body, mesh=mesh, in_specs=in_specs, out_specs=out_specs, check_vma=False)
```

profile of v0, /device:TPU:14, one launch (start us, length us, event | category | flops | bytes accessed | tf_op | source)
XLA Modules:
  0.0 437.1 jit_solution(3423635285913149859)
XLA Ops:
  9.7 7.1 %all-to-all-start.1 = ((s32[16,8,1]{1,2,0:T(1,128)}), s32[16,8,1]{1,2,0:T(1,128)S(1)}, u32[]{:S(2)}, u32[]{:S(2)}) async-start(s32[16,8,1]{1,2,0:T(1,128)} %bitcast.12), calls=%async_computation.1 | async-start | bytes 16384 | tf_op jit(solution)/shard_map/all_to_all | solution.py:62
  21.4 57.7 %all-gather.3.cloned.1.call-done = bf16[64,24576]{1,0:T(8,128)(2,1)} async-done(((bf16[64,1536]{1,0:T(8,128)(2,1)}), bf16[64,24576]{1,0:T(8,128)(2,1)}) %all-gather.3.cloned.1.call-update) | async-done | bytes 3145744 | tf_op jit(solution)/shard_map/all_gather | solution.py:87
  79.1 2.7 copy.52
  82.8 1.5 fusion.30
  84.4 3.7 psum.14
  88.2 4.5 %select_reduce_fusion.1 = f32[4,4096]{1,0:T(4,128)S(1)} fusion(f32[4,16,128]{2,1,0:T(8,128)S(1)} %psum.14, s32[4,4096]{1,0:T(4,128)S(1)} %get-tuple-element.4, s32[4,4096]{1,0:T(4,128)S(1)} %get-tuple-element.5), kind=kOutput, calls=%fused_computation.5 | convolution fusion | flops 409190400 | bytes 229376 | tf_op jit(solution)/shard_map/jwo,jom->jwm/dot_general | solution.py:106
  93.1 4.7 %fusion.2 = f32[4,16,128]{2,1,0:T(8,128)S(1)} fusion(f32[4,4096]{1,0:T(4,128)S(1)} %bitcast.142, s32[4,4096]{1,0:T(4,128)S(1)} %get-tuple-element.4, s32[4,4096]{1,0:T(4,128)S(1)} %get-tuple-element.5), kind=kOutput, calls=%fused_computation.3 | convolution fusion | flops 407109632 | bytes 229376 | tf_op jit(solution)/shard_map/boy,bom->bym/dot_general | solution.py:119
  97.8 8.8 %convolution_bitcast_fusion.1 = f32[64,128,128]{1,2,0:T(8,128)} fusion(f32[64,128]{1,0:T(8,128)S(1)} %bitcast.143, f32[64,64]{1,0:T(8,128)S(1)} %copy.30, s32[64]{0:T(128)S(1)} %multiply_add_fusion), kind=kOutput, calls=%fused_computation.18 | convolution fusion | flops 806379520 | bytes 4243712 | tf_op jit(solution)/shard_map/jn,knc->kjc/dot_general | solution.py:127
  106.6 5.4 %copy.32 = f32[64,128,128]{2,0,1:T(8,128)} copy(f32[64,128,128]{1,2,0:T(8,128)} %convolution_bitcast_fusion.1) | data formatting | bytes 8388608 | tf_op jit(solution)/shard_map/jn,knc->kjc/transpose | solution.py:127
  112.1 5.7 %all-to-all-start = ((f32[64,128,128]{2,0,1:T(8,128)}), f32[64,128,128]{2,0,1:T(8,128)}, u32[]{:S(2)}, u32[]{:S(2)}) async-start(f32[64,128,128]{2,0,1:T(8,128)} %copy.32), calls=%async_computation | async-start | bytes 8388608 | tf_op jit(solution)/shard_map/all_to_all | solution.py:128
  119.7 94.7 %all-to-all-done = f32[64,128,128]{2,0,1:T(8,128)} async-done(((f32[64,128,128]{2,0,1:T(8,128)}), f32[64,128,128]{2,0,1:T(8,128)}, u32[]{:S(2)}, u32[]{:S(2)}) %all-to-all-start) | async-done | bytes 4194336 | tf_op jit(solution)/shard_map/all_to_all | solution.py:128
  214.4 5.8 %fusion.6 = f32[64,128,12]{1,2,0:T(8,128)S(1)} fusion(f32[64,128,128]{2,0,1:T(8,128)} %all-to-all-done, s32[128]{0:T(128)S(1)} %eq.73), kind=kOutput, calls=%fused_computation.9 | convolution fusion | flops 150996480 | bytes 4588032 | tf_op jit(solution)/shard_map/qj,kjc->kqc/dot_general | solution.py:129
  222.5 65.6 %all-gather.5.cloned.1.call-done = bf16[64,24576]{1,0:T(8,128)(2,1)} async-done(((bf16[64,1536]{1,0:T(8,128)(2,1)}), bf16[64,24576]{1,0:T(8,128)(2,1)}) %all-gather.5.cloned.1.call-update) | async-done | bytes 3145744 | tf_op jit(solution)/shard_map/all_gather | solution.py:87
  288.1 2.7 copy.57
  291.9 1.5 fusion.26
  293.5 3.6 psum.15
  297.1 4.5 %select_reduce_fusion = f32[4,4096]{1,0:T(4,128)S(1)} fusion(f32[4,16,128]{2,1,0:T(8,128)S(1)} %psum.15, s32[4,4096]{1,0:T(4,128)S(1)} %get-tuple-element.4, s32[4,4096]{1,0:T(4,128)S(1)} %get-tuple-element.5), kind=kOutput, calls=%fused_computation.2 | convolution fusion | flops 409190400 | bytes 229376 | tf_op jit(solution)/shard_map/jwo,jom->jwm/dot_general | solution.py:106
  301.9 4.7 %fusion = f32[4,16,128]{2,1,0:T(8,128)S(1)} fusion(f32[4,4096]{1,0:T(4,128)S(1)} %bitcast.141, s32[4,4096]{1,0:T(4,128)S(1)} %get-tuple-element.4, s32[4,4096]{1,0:T(4,128)S(1)} %get-tuple-element.5), kind=kOutput, calls=%fused_computation | convolution fusion | flops 407109632 | bytes 229376 | tf_op jit(solution)/shard_map/boy,bom->bym/dot_general | solution.py:119
  306.7 8.8 %convolution_bitcast_fusion = f32[64,128,128]{1,2,0:T(8,128)} fusion(f32[64,128]{1,0:T(8,128)S(1)} %bitcast.145, f32[64,64]{1,0:T(8,128)S(1)} %copy.35, s32[64]{0:T(128)S(1)} %multiply_add_fusion), kind=kOutput, calls=%fused_computation.17 | convolution fusion | flops 806379520 | bytes 4243712 | tf_op jit(solution)/shard_map/jn,knc->kjc/dot_general | solution.py:127
  315.5 5.4 %copy.37 = f32[64,128,128]{2,0,1:T(8,128)} copy(f32[64,128,128]{1,2,0:T(8,128)} %convolution_bitcast_fusion) | data formatting | bytes 8388608 | tf_op jit(solution)/shard_map/jn,knc->kjc/transpose | solution.py:127
  320.9 6.1 %all-to-all-start.2 = ((f32[64,128,128]{2,0,1:T(8,128)}), f32[64,128,128]{2,0,1:T(8,128)}, u32[]{:S(2)}, u32[]{:S(2)}) async-start(f32[64,128,128]{2,0,1:T(8,128)} %copy.37), calls=%async_computation.2 | async-start | bytes 8388608 | tf_op jit(solution)/shard_map/all_to_all | solution.py:128
  327.0 1.3 fusion.24
  328.9 94.4 %all-to-all-done.2 = f32[64,128,128]{2,0,1:T(8,128)} async-done(((f32[64,128,128]{2,0,1:T(8,128)}), f32[64,128,128]{2,0,1:T(8,128)}, u32[]{:S(2)}, u32[]{:S(2)}) %all-to-all-start.2) | async-done | bytes 4194336 | tf_op jit(solution)/shard_map/all_to_all | solution.py:128
  423.3 5.8 %fusion.4 = f32[64,128,12]{1,2,0:T(8,128)S(1)} fusion(f32[64,128,128]{2,0,1:T(8,128)} %all-to-all-done.2, s32[128]{0:T(128)S(1)} %eq.73), kind=kOutput, calls=%fused_computation.7 | convolution fusion | flops 150996480 | bytes 4588032 | tf_op jit(solution)/shard_map/qj,kjc->kqc/dot_general | solution.py:129
  (65 shorter events, 15.5 us)
Async XLA Ops:
  7.2 71.9 %all-gather.3.cloned.1.call-start = ((), (), s32[]{:S(2)}) async-start(), calls=%async_computation.3 | async-start | bytes 3342336 | tf_op jit(solution)/shard_map/all_gather | solution.py:87
  9.7 102.4 %all-to-all-start.1 = ((s32[16,8,1]{1,2,0:T(1,128)}), s32[16,8,1]{1,2,0:T(1,128)S(1)}, u32[]{:S(2)}, u32[]{:S(2)}) async-start(s32[16,8,1]{1,2,0:T(1,128)} %bitcast.12), calls=%async_computation.1 | async-start | bytes 16384 | tf_op jit(solution)/shard_map/all_to_all | solution.py:62
  81.8 1.0 copy-start.5
  88.1 4.5 %copy-start.2 = (f32[4,32,128]{2,1,0:T(8,128)S(1)}, f32[4,32,128]{2,1,0:T(8,128)}, u32[]{:S(2)}) copy-start(f32[4,32,128]{2,1,0:T(8,128)} %param.11) | copy-start | bytes 196612
  88.1 4.5 %copy-start.3 = (s32[4]{0:T(128)S(1)}, s32[4]{0:T(128)}, u32[]{:S(2)}) copy-start(s32[4]{0:T(128)} %param.17) | copy-start | bytes 52
  88.1 4.5 %copy-start.4 = (s32[4]{0:T(128)S(1)}, s32[4]{0:T(128)}, u32[]{:S(2)}) copy-start(s32[4]{0:T(128)} %param.16) | copy-start | bytes 52
  88.2 4.5 %copy-start.6 = (f32[4]{0:T(128)S(1)}, f32[4]{0:T(128)}, u32[]{:S(2)}) copy-start(f32[4]{0:T(128)} %param.12) | copy-start | bytes 52
  88.2 4.7 %copy-start.7 = (f32[4]{0:T(128)S(1)}, f32[4]{0:T(128)}, u32[]{:S(2)}) copy-start(f32[4]{0:T(128)} %param.14) | copy-start | bytes 52
  112.1 102.3 %all-to-all-start = ((f32[64,128,128]{2,0,1:T(8,128)}), f32[64,128,128]{2,0,1:T(8,128)}, u32[]{:S(2)}, u32[]{:S(2)}) async-start(f32[64,128,128]{2,0,1:T(8,128)} %copy.32), calls=%async_computation | async-start | bytes 8388608 | tf_op jit(solution)/shard_map/all_to_all | solution.py:128
  117.8 102.4 %copy-start.1 = (bf16[64,1536]{1,0:T(8,128)(2,1)S(1)}, bf16[64,1536]{1,0:T(8,128)(2,1)}, u32[]{:S(2)}) copy-start(bf16[64,1536]{1,0:T(8,128)(2,1)} %param.19) | copy-start | bytes 589828
  117.8 102.4 %copy-start.8 = (f32[64]{0:T(128)S(1)}, f32[64]{0:T(128)}, u32[]{:S(2)}) copy-start(f32[64]{0:T(128)} %param.21) | copy-start | bytes 772
  117.8 170.3 %all-gather.5.cloned.1.call-start = ((), (), s32[]{:S(2)}) async-start(), calls=%async_computation.4 | async-start | bytes 3342336 | tf_op jit(solution)/shard_map/all_gather | solution.py:87
  320.9 102.4 %all-to-all-start.2 = ((f32[64,128,128]{2,0,1:T(8,128)}), f32[64,128,128]{2,0,1:T(8,128)}, u32[]{:S(2)}, u32[]{:S(2)}) async-start(f32[64,128,128]{2,0,1:T(8,128)} %copy.37), calls=%async_computation.2 | async-start | bytes 8388608 | tf_op jit(solution)/shard_map/all_to_all | solution.py:128
  327.0 102.1 %copy-start = (bf16[64,1536]{1,0:T(8,128)(2,1)S(1)}, bf16[64,1536]{1,0:T(8,128)(2,1)}, u32[]{:S(2)}) copy-start(bf16[64,1536]{1,0:T(8,128)(2,1)} %fusion.38) | copy-start | bytes 589828
Sparse Core Ops, SparseCore 0:
  10.7 68.3 all-gather.2
  221.3 66.8 all-gather.4
where the time goes:
time: 441 us; the launch traced here: 437 us
  waiting for transfers between devices  313 us (71%)
  matrix products  54.7 us (12%)
  local copies, waits for them, and re-layouts  20.7 us (5%)
  starting transfers between devices  19.6 us (4%)
  between operations  14.6 us (3%)
  blocking collectives  7.28 us (2%)
  other arithmetic  7.07 us (2%)
    all_to_all x2, waiting for transfers between devices, evaluate(): lax.all_to_all(outgoing, 'trial', split_axis=1, concat_axis=1, tiled=True)  189 us
    all_gather x2, waiting for transfers between devices, fetch(): whole = lax.all_gather(current, 'trial', axis=1, tiled=True)  123 us
    dot_general x2, matrix products, evaluate(): jnp.einsum('jn,knc->kjc', placer, returned, precision=lax.Precision.HIGHEST)  17.7 us
    all_to_all x2, starting transfers between devices, evaluate(): lax.all_to_all(outgoing, 'trial', split_axis=1, concat_axis=1, tiled=True)  11.8 us
    dot_general x2, matrix products, evaluate(): jnp.einsum('qj,kjc->kqc', picker, arrived, precision=lax.Precision.HIGHEST)  11.6 us
    transpose x2, local copies, waits for them, and re-layouts, evaluate(): jnp.einsum('jn,knc->kjc', placer, returned, precision=lax.Precision.HIGHEST)  10.8 us
    dot_general x2, matrix products, evaluate(): jnp.einsum('boy,bom->bym', panel_onehot_matrix, dispersion_amount, precis...  9.44 us
    dot_general x2, matrix products, evaluate(): jnp.einsum('jwo,jom->jwm', panel_onehot_matrix, effect_table_grid, precis...  8.93 us
  transfers between devices with their start and end apart: 5, of which 4 were waited for; matrix products, arithmetic and copies ran while one was open for 9% of the time, Pallas kernels for 0%

commit v1 on v0

--- a/solution.py
+++ b/solution.py
@@ -6,6 +6,19 @@
 PANEL = 128
 score_step = 0.005
 load_step = 0.02
+
+
+def gather_around(array, axis, dim):
+    ways = lax.axis_size(axis)
+    up = [(d, (d + 1) % ways) for d in range(ways)]
+    down = [(d, (d - 1) % ways) for d in range(ways)]
+    earlier, later = ([array], [array])
+    for _ in range(ways // 2):
+        earlier.append(lax.ppermute(earlier[-1], axis, up))
+    for _ in range((ways - 1) // 2):
+        later.append(lax.ppermute(later[-1], axis, down))
+    line = jnp.concatenate([*earlier[::-1], *later[1:]], axis=dim)
+    return jnp.roll(line, (lax.axis_index(axis) - ways // 2) * array.shape[dim], axis=dim)
 
 
 def sweep_axis(values_in, corr_value, position, limit_count, axis_number):
@@ -84,7 +97,7 @@
     corr_cols = correlations[:, 1][:, None, None]
 
     def fetch(current):
-        whole = lax.all_gather(current, "trial", axis=1, tiled=True)
+        whole = gather_around(current, "trial", 1)
         grouped = whole.reshape(latent_factor_count, -1, PANEL)
         panel_total = grouped.shape[1]
         chooser = (

time: 441 us -> 455 us (1.032)
  starting transfers between devices: 19.6 us -> 84.7 us
  waiting for transfers between devices: 313 us -> 269 us
  between operations: 14.6 us -> 1.93 us
    all_gather x2 -> x0, waiting for transfers between devices: 123 us -> none  [fetch(): whole = lax.all_gather(current, 'trial', axis=1, tiled=True)]
    ppermute x0 -> x30, waiting for transfers between devices: none -> 81.2 us  [the longest x16 40.9 us: gather_around(): earlier.append(lax.ppermute(earlier[-1], axis, up))]
    ppermute x0 -> x30, starting transfers between devices: none -> 52 us  [the longest x14 27.6 us: gather_around(): later.append(lax.ppermute(later[-1], axis, down))]
    all_to_all x2, starting transfers between devices: 11.8 us -> 27.2 us  [evaluate(): lax.all_to_all(outgoing, 'trial', split_axis=1, concat_axis=1, tiled=True)]
    unnamed x2 -> x4, other arithmetic: 0.21 us -> 4.99 us
  transfers between devices with their start and end apart: 5 -> 33, of which waited for: 4 -> 25; matrix products, arithmetic and copies ran while one was open for 9% -> 9% of each run, Pallas kernels for 0% -> 0%
where the time goes in v1:
time: 455 us; the launch traced here: 448 us
  waiting for transfers between devices  269 us (59%)
  starting transfers between devices  84.7 us (19%)
  matrix products  54.8 us (12%)
  local copies, waits for them, and re-layouts  19 us (4%)
  other arithmetic  11.1 us (2%)
  blocking collectives  7.39 us (2%)
    all_to_all x2, waiting for transfers between devices, evaluate(): lax.all_to_all(outgoing, 'trial', split_axis=1, concat_axis=1, tiled=True)  188 us
    ppermute x16, waiting for transfers between devices, gather_around(): earlier.append(lax.ppermute(earlier[-1], axis, up))  40.9 us
    ppermute x14, waiting for transfers between devices, gather_around(): later.append(lax.ppermute(later[-1], axis, down))  40.3 us
    ppermute x14, starting transfers between devices, gather_around(): later.append(lax.ppermute(later[-1], axis, down))  27.6 us
    all_to_all x2, starting transfers between devices, evaluate(): lax.all_to_all(outgoing, 'trial', split_axis=1, concat_axis=1, tiled=True)  27.2 us
    ppermute x16, starting transfers between devices, gather_around(): earlier.append(lax.ppermute(earlier[-1], axis, up))  24.5 us
    dot_general x2, matrix products, evaluate(): jnp.einsum('jn,knc->kjc', placer, returned, precision=lax.Precision.HIGHEST)  17.7 us
    dot_general x2, matrix products, evaluate(): jnp.einsum('qj,kjc->kqc', picker, arrived, precision=lax.Precision.HIGHEST)  11.6 us
  transfers between devices with their start and end apart: 33, of which 25 were waited for; matrix products, arithmetic and copies ran while one was open for 9% of the time, Pallas kernels for 0%

profile of v1, /device:TPU:14, one launch (start us, length us, event | category | flops | bytes accessed | tf_op | source)
XLA Modules:
  0.0 448.0 jit_solution(11430789534005772794)
XLA Ops:
  3.8 4.9 %collective-permute-done = bf16[64,1536]{1,0:T(8,128)(2,1)S(1)} collective-permute-done((bf16[64,1536]{1,0:T(8,128)(2,1)}, bf16[64,1536]{1,0:T(8,128)(2,1)S(1)}, u32[]{:S(2)}, u32[]{:S(2)}) %collective-permute-start) | collective-permute-done | bytes 196640 | tf_op jit(solution)/shard_map/ppermute | solution.py:17
  8.7 4.7 %collective-permute-start.1 = (bf16[64,1536]{1,0:T(8,128)(2,1)S(1)}, bf16[64,1536]{1,0:T(8,128)(2,1)S(1)}, u32[]{:S(2)}, u32[]{:S(2)}) collective-permute-start(bf16[64,1536]{1,0:T(8,128)(2,1)S(1)} %collective-permute-done), channel_id=1, source_target_pairs={{0,2},{2,4},{4,6},{6,8},{8,10},{10,12},{12,14},{14,16},{16,18},{18... | collective-permute-start | bytes 589832 | tf_op jit(solution)/shard_map/ppermute | solution.py:17
  14.0 5.5 %all-to-all-start.1 = ((s32[16,8,1]{1,2,0:T(1,128)}), s32[16,8,1]{1,2,0:T(1,128)S(1)}, u32[]{:S(2)}, u32[]{:S(2)}) async-start(s32[16,8,1]{1,2,0:T(1,128)} %bitcast.12), calls=%async_computation.1 | async-start | bytes 16384 | tf_op jit(solution)/shard_map/all_to_all | solution.py:75
  36.9 4.5 %collective-permute-done.10 = bf16[64,1536]{1,0:T(8,128)(2,1)S(1)} collective-permute-done((bf16[64,1536]{1,0:T(8,128)(2,1)S(1)}, bf16[64,1536]{1,0:T(8,128)(2,1)S(1)}, u32[]{:S(2)}, u32[]{:S(2)}) %collective-permute-start.10) | collective-permute-done | bytes 196640 | tf_op jit(solution)/shard_map/ppermute | solution.py:19
  46.1 5.6 %collective-permute-done.11 = bf16[64,1536]{1,0:T(8,128)(2,1)S(1)} collective-permute-done((bf16[64,1536]{1,0:T(8,128)(2,1)S(1)}, bf16[64,1536]{1,0:T(8,128)(2,1)S(1)}, u32[]{:S(2)}, u32[]{:S(2)}) %collective-permute-start.11) | collective-permute-done | bytes 196640 | tf_op jit(solution)/shard_map/ppermute | solution.py:19
  57.8 5.7 %collective-permute-done.12 = bf16[64,1536]{1,0:T(8,128)(2,1)S(1)} collective-permute-done((bf16[64,1536]{1,0:T(8,128)(2,1)S(1)}, bf16[64,1536]{1,0:T(8,128)(2,1)S(1)}, u32[]{:S(2)}, u32[]{:S(2)}) %collective-permute-start.12) | collective-permute-done | bytes 196640 | tf_op jit(solution)/shard_map/ppermute | solution.py:19
  75.4 4.7 %collective-permute-done.14 = bf16[64,1536]{1,0:T(8,128)(2,1)S(1)} collective-permute-done((bf16[64,1536]{1,0:T(8,128)(2,1)S(1)}, bf16[64,1536]{1,0:T(8,128)(2,1)S(1)}, u32[]{:S(2)}, u32[]{:S(2)}) %collective-permute-start.14) | collective-permute-done | bytes 196640 | tf_op jit(solution)/shard_map/ppermute | solution.py:19
  94.7 4.7 %fusion.2 = f32[4,16,128]{2,1,0:T(8,128)S(1)} fusion(f32[4,4096]{1,0:T(4,128)S(1)} %bitcast.142, s32[4,4096]{1,0:T(4,128)S(1)} %get-tuple-element.5, s32[4,4096]{1,0:T(4,128)S(1)} %get-tuple-element.6), kind=kOutput, calls=%fused_computation.3 | convolution fusion | flops 407109632 | bytes 229376 | tf_op jit(solution)/shard_map/boy,bom->bym/dot_general | solution.py:132
  99.4 8.9 %convolution_bitcast_fusion.1 = f32[64,128,128]{1,2,0:T(8,128)} fusion(f32[64,128]{1,0:T(8,128)S(1)} %bitcast.143, f32[64,64]{1,0:T(8,128)S(1)} %copy.30, s32[64]{0:T(128)S(1)} %multiply_add_fusion), kind=kOutput, calls=%fused_computation.26 | convolution fusion | flops 806379520 | bytes 4243712 | tf_op jit(solution)/shard_map/jn,knc->kjc/dot_general | solution.py:140
  108.3 5.4 %copy.32 = f32[64,128,128]{2,0,1:T(8,128)} copy(f32[64,128,128]{1,2,0:T(8,128)} %convolution_bitcast_fusion.1) | data formatting | bytes 8388608 | tf_op jit(solution)/shard_map/jn,knc->kjc/transpose | solution.py:140
  113.7 13.0 %all-to-all-start = ((f32[64,128,128]{2,0,1:T(8,128)}), f32[64,128,128]{2,0,1:T(8,128)}, u32[]{:S(2)}, u32[]{:S(2)}) async-start(f32[64,128,128]{2,0,1:T(8,128)} %copy.32), calls=%async_computation | async-start | bytes 8388608 | tf_op jit(solution)/shard_map/all_to_all | solution.py:141
  128.0 94.3 %all-to-all-done = f32[64,128,128]{2,0,1:T(8,128)} async-done(((f32[64,128,128]{2,0,1:T(8,128)}), f32[64,128,128]{2,0,1:T(8,128)}, u32[]{:S(2)}, u32[]{:S(2)}) %all-to-all-start) | async-done | bytes 4194336 | tf_op jit(solution)/shard_map/all_to_all | solution.py:141
  222.3 5.8 %fusion.6 = f32[64,128,12]{1,2,0:T(8,128)S(1)} fusion(f32[64,128,128]{2,0,1:T(8,128)} %all-to-all-done, s32[128]{0:T(128)S(1)} %eq.75), kind=kOutput, calls=%fused_computation.13 | convolution fusion | flops 150996480 | bytes 4588032 | tf_op jit(solution)/shard_map/qj,kjc->kqc/dot_general | solution.py:142
  228.4 6.0 %collective-permute-done.15 = bf16[64,1536]{1,0:T(8,128)(2,1)S(1)} collective-permute-done((bf16[64,1536]{1,0:T(8,128)(2,1)S(1)}, bf16[64,1536]{1,0:T(8,128)(2,1)S(1)}, u32[]{:S(2)}, u32[]{:S(2)}) %collective-permute-start.15) | collective-permute-done | bytes 196640 | tf_op jit(solution)/shard_map/ppermute | solution.py:17
  236.5 5.8 %collective-permute-done.16 = bf16[64,1536]{1,0:T(8,128)(2,1)S(1)} collective-permute-done((bf16[64,1536]{1,0:T(8,128)(2,1)S(1)}, bf16[64,1536]{1,0:T(8,128)(2,1)S(1)}, u32[]{:S(2)}, u32[]{:S(2)}) %collective-permute-start.16) | collective-permute-done | bytes 196640 | tf_op jit(solution)/shard_map/ppermute | solution.py:17
  254.7 4.7 %collective-permute-done.18 = bf16[64,1536]{1,0:T(8,128)(2,1)S(1)} collective-permute-done((bf16[64,1536]{1,0:T(8,128)(2,1)S(1)}, bf16[64,1536]{1,0:T(8,128)(2,1)S(1)}, u32[]{:S(2)}, u32[]{:S(2)}) %collective-permute-start.18) | collective-permute-done | bytes 196640 | tf_op jit(solution)/shard_map/ppermute | solution.py:17
  262.7 4.7 %collective-permute-done.19 = bf16[64,1536]{1,0:T(8,128)(2,1)S(1)} collective-permute-done((bf16[64,1536]{1,0:T(8,128)(2,1)S(1)}, bf16[64,1536]{1,0:T(8,128)(2,1)S(1)}, u32[]{:S(2)}, u32[]{:S(2)}) %collective-permute-start.19) | collective-permute-done | bytes 196640 | tf_op jit(solution)/shard_map/ppermute | solution.py:17
  271.1 5.0 %collective-permute-done.20 = bf16[64,1536]{1,0:T(8,128)(2,1)S(1)} collective-permute-done((bf16[64,1536]{1,0:T(8,128)(2,1)S(1)}, bf16[64,1536]{1,0:T(8,128)(2,1)S(1)}, u32[]{:S(2)}, u32[]{:S(2)}) %collective-permute-start.20) | collective-permute-done | bytes 196640 | tf_op jit(solution)/shard_map/ppermute | solution.py:17
  312.4 4.7 %fusion = f32[4,16,128]{2,1,0:T(8,128)S(1)} fusion(f32[4,4096]{1,0:T(4,128)S(1)} %bitcast.141, s32[4,4096]{1,0:T(4,128)S(1)} %copy-done.4, s32[4,4096]{1,0:T(4,128)S(1)} %copy-done.6), kind=kOutput, calls=%fused_computation | convolution fusion | flops 407109632 | bytes 229376 | tf_op jit(solution)/shard_map/boy,bom->bym/dot_general | solution.py:132
  317.1 8.9 %convolution_bitcast_fusion = f32[64,128,128]{1,2,0:T(8,128)} fusion(f32[64,128]{1,0:T(8,128)S(1)} %bitcast.145, f32[64,64]{1,0:T(8,128)S(1)} %copy-done.2, s32[64]{0:T(128)S(1)} %copy-done.33), kind=kOutput, calls=%fused_computation.25 | convolution fusion | flops 806379520 | bytes 4243712 | tf_op jit(solution)/shard_map/jn,knc->kjc/dot_general | solution.py:140
  326.0 5.4 %copy.37 = f32[64,128,128]{2,0,1:T(8,128)} copy(f32[64,128,128]{1,2,0:T(8,128)} %convolution_bitcast_fusion) | data formatting | bytes 8388608 | tf_op jit(solution)/shard_map/jn,knc->kjc/transpose | solution.py:140
  331.4 14.1 %all-to-all-start.2 = ((f32[64,128,128]{2,0,1:T(8,128)}), f32[64,128,128]{2,0,1:T(8,128)}, u32[]{:S(2)}, u32[]{:S(2)}) async-start(f32[64,128,128]{2,0,1:T(8,128)} %copy.37), calls=%async_computation.2 | async-start | bytes 8388608 | tf_op jit(solution)/shard_map/all_to_all | solution.py:141
  347.4 93.7 %all-to-all-done.2 = f32[64,128,128]{2,0,1:T(8,128)} async-done(((f32[64,128,128]{2,0,1:T(8,128)}), f32[64,128,128]{2,0,1:T(8,128)}, u32[]{:S(2)}, u32[]{:S(2)}) %all-to-all-start.2) | async-done | bytes 4194336 | tf_op jit(solution)/shard_map/all_to_all | solution.py:141
  441.1 5.8 %fusion.4 = f32[64,128,12]{1,2,0:T(8,128)S(1)} fusion(f32[64,128,128]{2,0,1:T(8,128)} %all-to-all-done.2, s32[128]{0:T(128)S(1)} %copy-done.13), kind=kOutput, calls=%fused_computation.11 | convolution fusion | flops 150996480 | bytes 4588032 | tf_op jit(solution)/shard_map/qj,kjc->kqc/dot_general | solution.py:142
  (219 shorter events, 119.8 us)
Async XLA Ops:
  0.6 8.1 %collective-permute-start = (bf16[64,1536]{1,0:T(8,128)(2,1)}, bf16[64,1536]{1,0:T(8,128)(2,1)S(1)}, u32[]{:S(2)}, u32[]{:S(2)}) collective-permute-start(bf16[64,1536]{1,0:T(8,128)(2,1)} %param.21), channel_id=1, source_target_pairs={{0,2},{2,4},{4,6},{6,8},{8,10},{10,12},{12,14},{14,16},{16,18},{18... | collective-permute-start | bytes 589832 | tf_op jit(solution)/shard_map/ppermute | solution.py:17
  2.2 20.6 %collective-permute-start.8 = (bf16[64,1536]{1,0:T(8,128)(2,1)}, bf16[64,1536]{1,0:T(8,128)(2,1)S(1)}, u32[]{:S(2)}, u32[]{:S(2)}) collective-permute-start(bf16[64,1536]{1,0:T(8,128)(2,1)} %param.21), channel_id=1, source_target_pairs={{0,30},{2,0},{4,2},{6,4},{8,6},{10,8},{12,10},{14,12},{16,14},{18,... | collective-permute-start | bytes 589832 | tf_op jit(solution)/shard_map/ppermute | solution.py:19
  8.7 10.8 %collective-permute-start.1 = (bf16[64,1536]{1,0:T(8,128)(2,1)S(1)}, bf16[64,1536]{1,0:T(8,128)(2,1)S(1)}, u32[]{:S(2)}, u32[]{:S(2)}) collective-permute-start(bf16[64,1536]{1,0:T(8,128)(2,1)S(1)} %collective-permute-done), channel_id=1, source_target_pairs={{0,2},{2,4},{4,6},{6,8},{8,10},{10,12},{12,14},{14,16},{16,18},{18... | collective-permute-start | bytes 589832 | tf_op jit(solution)/shard_map/ppermute | solution.py:17
  14.0 99.6 %all-to-all-start.1 = ((s32[16,8,1]{1,2,0:T(1,128)}), s32[16,8,1]{1,2,0:T(1,128)S(1)}, u32[]{:S(2)}, u32[]{:S(2)}) async-start(s32[16,8,1]{1,2,0:T(1,128)} %bitcast.12), calls=%async_computation.1 | async-start | bytes 16384 | tf_op jit(solution)/shard_map/all_to_all | solution.py:75
  22.8 9.3 %collective-permute-start.9 = (bf16[64,1536]{1,0:T(8,128)(2,1)S(1)}, bf16[64,1536]{1,0:T(8,128)(2,1)S(1)}, u32[]{:S(2)}, u32[]{:S(2)}) collective-permute-start(bf16[64,1536]{1,0:T(8,128)(2,1)S(1)} %collective-permute-done.8), channel_id=1, source_target_pairs={{0,30},{2,0},{4,2},{6,4},{8,6},{10,8},{12,10},{14,12},{16,14},{18,... | collective-permute-start | bytes 589832 | tf_op jit(solution)/shard_map/ppermute | solution.py:19
  32.1 9.4 %collective-permute-start.10 = (bf16[64,1536]{1,0:T(8,128)(2,1)S(1)}, bf16[64,1536]{1,0:T(8,128)(2,1)S(1)}, u32[]{:S(2)}, u32[]{:S(2)}) collective-permute-start(bf16[64,1536]{1,0:T(8,128)(2,1)S(1)} %collective-permute-done.9), channel_id=1, source_target_pairs={{0,30},{2,0},{4,2},{6,4},{8,6},{10,8},{12,10},{14,12},{16,14},{18,... | collective-permute-start | bytes 589832 | tf_op jit(solution)/shard_map/ppermute | solution.py:19
  34.9 9.1 %collective-permute-start.4 = (bf16[64,1536]{1,0:T(8,128)(2,1)S(1)}, bf16[64,1536]{1,0:T(8,128)(2,1)S(1)}, u32[]{:S(2)}, u32[]{:S(2)}) collective-permute-start(bf16[64,1536]{1,0:T(8,128)(2,1)S(1)} %collective-permute-done.3), channel_id=1, source_target_pairs={{0,2},{2,4},{4,6},{6,8},{8,10},{10,12},{12,14},{14,16},{16,18},{18... | collective-permute-start | bytes 589832 | tf_op jit(solution)/shard_map/ppermute | solution.py:17
  41.5 10.3 %collective-permute-start.11 = (bf16[64,1536]{1,0:T(8,128)(2,1)S(1)}, bf16[64,1536]{1,0:T(8,128)(2,1)S(1)}, u32[]{:S(2)}, u32[]{:S(2)}) collective-permute-start(bf16[64,1536]{1,0:T(8,128)(2,1)S(1)} %collective-permute-done.10), channel_id=1, source_target_pairs={{0,30},{2,0},{4,2},{6,4},{8,6},{10,8},{12,10},{14,12},{16,14},{18,... | collective-permute-start | bytes 589832 | tf_op jit(solution)/shard_map/ppermute | solution.py:19
  44.0 10.4 %collective-permute-start.5 = (bf16[64,1536]{1,0:T(8,128)(2,1)S(1)}, bf16[64,1536]{1,0:T(8,128)(2,1)S(1)}, u32[]{:S(2)}, u32[]{:S(2)}) collective-permute-start(bf16[64,1536]{1,0:T(8,128)(2,1)S(1)} %collective-permute-done.4), channel_id=1, source_target_pairs={{0,2},{2,4},{4,6},{6,8},{8,10},{10,12},{12,14},{14,16},{16,18},{18... | collective-permute-start | bytes 589832 | tf_op jit(solution)/shard_map/ppermute | solution.py:17
  51.7 11.8 %collective-permute-start.12 = (bf16[64,1536]{1,0:T(8,128)(2,1)S(1)}, bf16[64,1536]{1,0:T(8,128)(2,1)S(1)}, u32[]{:S(2)}, u32[]{:S(2)}) collective-permute-start(bf16[64,1536]{1,0:T(8,128)(2,1)S(1)} %collective-permute-done.11), channel_id=1, source_target_pairs={{0,30},{2,0},{4,2},{6,4},{8,6},{10,8},{12,10},{14,12},{16,14},{18,... | collective-permute-start | bytes 589832 | tf_op jit(solution)/shard_map/ppermute | solution.py:19
  54.4 11.6 %collective-permute-start.6 = (bf16[64,1536]{1,0:T(8,128)(2,1)S(1)}, bf16[64,1536]{1,0:T(8,128)(2,1)S(1)}, u32[]{:S(2)}, u32[]{:S(2)}) collective-permute-start(bf16[64,1536]{1,0:T(8,128)(2,1)S(1)} %collective-permute-done.5), channel_id=1, source_target_pairs={{0,2},{2,4},{4,6},{6,8},{8,10},{10,12},{12,14},{14,16},{16,18},{18... | collective-permute-start | bytes 589832 | tf_op jit(solution)/shard_map/ppermute | solution.py:17
  63.5 9.2 %collective-permute-start.13 = (bf16[64,1536]{1,0:T(8,128)(2,1)S(1)}, bf16[64,1536]{1,0:T(8,128)(2,1)S(1)}, u32[]{:S(2)}, u32[]{:S(2)}) collective-permute-start(bf16[64,1536]{1,0:T(8,128)(2,1)S(1)} %collective-permute-done.12), channel_id=1, source_target_pairs={{0,30},{2,0},{4,2},{6,4},{8,6},{10,8},{12,10},{14,12},{16,14},{18,... | collective-permute-start | bytes 589832 | tf_op jit(solution)/shard_map/ppermute | solution.py:19
  66.0 9.1 %collective-permute-start.7 = (bf16[64,1536]{1,0:T(8,128)(2,1)S(1)}, bf16[64,1536]{1,0:T(8,128)(2,1)S(1)}, u32[]{:S(2)}, u32[]{:S(2)}) collective-permute-start(bf16[64,1536]{1,0:T(8,128)(2,1)S(1)} %collective-permute-done.6), channel_id=1, source_target_pairs={{0,2},{2,4},{4,6},{6,8},{8,10},{10,12},{12,14},{14,16},{16,18},{18... | collective-permute-start | bytes 589832 | tf_op jit(solution)/shard_map/ppermute | solution.py:17
  113.7 108.6 %all-to-all-start = ((f32[64,128,128]{2,0,1:T(8,128)}), f32[64,128,128]{2,0,1:T(8,128)}, u32[]{:S(2)}, u32[]{:S(2)}) async-start(f32[64,128,128]{2,0,1:T(8,128)} %copy.32), calls=%async_computation | async-start | bytes 8388608 | tf_op jit(solution)/shard_map/all_to_all | solution.py:141
  236.5 8.9 %collective-permute-start.23 = (bf16[64,1536]{1,0:T(8,128)(2,1)S(1)}, bf16[64,1536]{1,0:T(8,128)(2,1)S(1)}, u32[]{:S(2)}, u32[]{:S(2)}) collective-permute-start(bf16[64,1536]{1,0:T(8,128)(2,1)S(1)} %fusion.42), channel_id=1, source_target_pairs={{0,30},{2,0},{4,2},{6,4},{8,6},{10,8},{12,10},{14,12},{16,14},{18,... | collective-permute-start | bytes 589832 | tf_op jit(solution)/shard_map/ppermute | solution.py:19
  242.2 8.4 %collective-permute-start.17 = (bf16[64,1536]{1,0:T(8,128)(2,1)S(1)}, bf16[64,1536]{1,0:T(8,128)(2,1)S(1)}, u32[]{:S(2)}, u32[]{:S(2)}) collective-permute-start(bf16[64,1536]{1,0:T(8,128)(2,1)S(1)} %collective-permute-done.16), channel_id=1, source_target_pairs={{0,2},{2,4},{4,6},{6,8},{8,10},{10,12},{12,14},{14,16},{16,18},{18... | collective-permute-start | bytes 589832 | tf_op jit(solution)/shard_map/ppermute | solution.py:17
  250.7 8.7 %collective-permute-start.18 = (bf16[64,1536]{1,0:T(8,128)(2,1)S(1)}, bf16[64,1536]{1,0:T(8,128)(2,1)S(1)}, u32[]{:S(2)}, u32[]{:S(2)}) collective-permute-start(bf16[64,1536]{1,0:T(8,128)(2,1)S(1)} %collective-permute-done.17), channel_id=1, source_target_pairs={{0,2},{2,4},{4,6},{6,8},{8,10},{10,12},{12,14},{14,16},{16,18},{18... | collective-permute-start | bytes 589832 | tf_op jit(solution)/shard_map/ppermute | solution.py:17
  259.4 8.0 %collective-permute-start.19 = (bf16[64,1536]{1,0:T(8,128)(2,1)S(1)}, bf16[64,1536]{1,0:T(8,128)(2,1)S(1)}, u32[]{:S(2)}, u32[]{:S(2)}) collective-permute-start(bf16[64,1536]{1,0:T(8,128)(2,1)S(1)} %collective-permute-done.18), channel_id=1, source_target_pairs={{0,2},{2,4},{4,6},{6,8},{8,10},{10,12},{12,14},{14,16},{16,18},{18... | collective-permute-start | bytes 589832 | tf_op jit(solution)/shard_map/ppermute | solution.py:17
  260.5 8.0 %collective-permute-start.26 = (bf16[64,1536]{1,0:T(8,128)(2,1)S(1)}, bf16[64,1536]{1,0:T(8,128)(2,1)S(1)}, u32[]{:S(2)}, u32[]{:S(2)}) collective-permute-start(bf16[64,1536]{1,0:T(8,128)(2,1)S(1)} %collective-permute-done.25), channel_id=1, source_target_pairs={{0,30},{2,0},{4,2},{6,4},{8,6},{10,8},{12,10},{14,12},{16,14},{18,... | collective-permute-start | bytes 589832 | tf_op jit(solution)/shard_map/ppermute | solution.py:19
  267.4 8.7 %collective-permute-start.20 = (bf16[64,1536]{1,0:T(8,128)(2,1)S(1)}, bf16[64,1536]{1,0:T(8,128)(2,1)S(1)}, u32[]{:S(2)}, u32[]{:S(2)}) collective-permute-start(bf16[64,1536]{1,0:T(8,128)(2,1)S(1)} %collective-permute-done.19), channel_id=1, source_target_pairs={{0,2},{2,4},{4,6},{6,8},{8,10},{10,12},{12,14},{14,16},{16,18},{18... | collective-permute-start | bytes 589832 | tf_op jit(solution)/shard_map/ppermute | solution.py:17
  268.6 11.7 %collective-permute-start.27 = (bf16[64,1536]{1,0:T(8,128)(2,1)S(1)}, bf16[64,1536]{1,0:T(8,128)(2,1)S(1)}, u32[]{:S(2)}, u32[]{:S(2)}) collective-permute-start(bf16[64,1536]{1,0:T(8,128)(2,1)S(1)} %collective-permute-done.26), channel_id=1, source_target_pairs={{0,30},{2,0},{4,2},{6,4},{8,6},{10,8},{12,10},{14,12},{16,14},{18,... | collective-permute-start | bytes 589832 | tf_op jit(solution)/shard_map/ppermute | solution.py:19
  276.0 9.7 %collective-permute-start.21 = (bf16[64,1536]{1,0:T(8,128)(2,1)S(1)}, bf16[64,1536]{1,0:T(8,128)(2,1)}, u32[]{:S(2)}, u32[]{:S(2)}) collective-permute-start(bf16[64,1536]{1,0:T(8,128)(2,1)S(1)} %collective-permute-done.20), channel_id=1, source_target_pairs={{0,2},{2,4},{4,6},{6,8},{8,10},{10,12},{12,14},{14,16},{16,18},{18... | collective-permute-start | bytes 589832 | tf_op jit(solution)/shard_map/ppermute | solution.py:17
  280.2 9.5 %collective-permute-start.28 = (bf16[64,1536]{1,0:T(8,128)(2,1)S(1)}, bf16[64,1536]{1,0:T(8,128)(2,1)S(1)}, u32[]{:S(2)}, u32[]{:S(2)}) collective-permute-start(bf16[64,1536]{1,0:T(8,128)(2,1)S(1)} %collective-permute-done.27), channel_id=1, source_target_pairs={{0,30},{2,0},{4,2},{6,4},{8,6},{10,8},{12,10},{14,12},{16,14},{18,... | collective-permute-start | bytes 589832 | tf_op jit(solution)/shard_map/ppermute | solution.py:19
  331.4 109.7 %all-to-all-start.2 = ((f32[64,128,128]{2,0,1:T(8,128)}), f32[64,128,128]{2,0,1:T(8,128)}, u32[]{:S(2)}, u32[]{:S(2)}) async-start(f32[64,128,128]{2,0,1:T(8,128)} %copy.37), calls=%async_computation.2 | async-start | bytes 8388608 | tf_op jit(solution)/shard_map/all_to_all | solution.py:141
  (51 other events, 1549.2 us)
